TPU v7x, 32 devices: a whole 2x2x4 slice. The times are simulated.
32 devices in a mesh: dp: 4 (over y, x), depth: 4 (over z), grid: 2 (over core).
Axes of the slice: x: 2, y: 2, z: 4, core: 2. Of those that a mesh axis runs over, the one named last changes fastest.
Arguments:
- tokens: bfloat16 [1024, 12288], P(('dp', 'depth'), 'grid'), may hold values from -6 to 6
- weight: bfloat16 [12288, 24576], P('grid', 'depth'), may hold values from -0.0546875 to 0.0546875
- cotangent: bfloat16 [1024, 24576], P(('dp', 'grid'), 'depth'), may hold values from -0.5 to 0.5
Outputs:
- hidden: bfloat16 [1024, 24576], P(('dp', 'grid'), 'depth')
- weight_grad: bfloat16 [12288, 24576], P(('grid', 'dp'), 'depth')
All inputs are finite; a program needn't handle non-finite values.
Results may differ from a plain program's by a relative error of at most 0.011.
Values may be sent and summed in bfloat16 or wider, within the bound.
No kernel may reach another device: no remote copies, remote signals or barrier semaphores. Data moves between devices by JAX's collectives and lax.ppermute only.
A program may use at most 192 MiB of HBM per device.

v0:
```python
import jax
import jax.numpy as jnp
from jax import lax
from jax.sharding import PartitionSpec as P


def gelu_tanh(values):
    return jax.nn.gelu(values, approximate=True)


def transposed_product(left, right):
    return lax.dot_general(
        left, right, (((0,), (0,)), ((), ())), preferred_element_type=jnp.float32
    )


def local(tokens, weight, cotangent):
    all_rows = lax.all_gather(tokens, ("dp", "depth"), axis=0, tiled=True)
    group_size = all_rows.shape[0] // lax.axis_size("dp")
    own_rows = lax.dynamic_slice_in_dim(all_rows, lax.axis_index("dp") * group_size, group_size, 0)
    partial_pre = jnp.dot(own_rows, weight, preferred_element_type=jnp.float32)
    preact = lax.psum_scatter(partial_pre, "grid", scatter_dimension=0, tiled=True)
    activated, pullback = jax.vjp(gelu_tanh, preact)
    hidden = activated.astype(jnp.bfloat16)
    grad_pre = pullback(cotangent.astype(jnp.float32))[0].astype(jnp.bfloat16)
    sub_width = all_rows.shape[1] // lax.axis_size("dp")
    columns = lax.dynamic_slice_in_dim(all_rows, lax.axis_index("dp") * sub_width, sub_width, 1)
    weight_grad = transposed_product(
        columns, lax.all_gather(grad_pre, ("dp", "grid"), axis=0, tiled=True)
    )
    return (hidden, weight_grad.astype(jnp.bfloat16))


def solution(mesh):
    return jax.shard_map(
        local,
        mesh=mesh,
        in_specs=(P(("dp", "depth"), "grid"), P("grid", "depth"), P(("dp", "grid"), "depth")),
        out_specs=(P(("dp", "grid"), "depth"), P(("grid", "dp"), "depth")),
        check_vma=False,
    )
```

profile of v0, /device:TPU:0, one launch (start us, length us, event | category | flops | bytes accessed | tf_op | source)
XLA Modules:
  0.0 322.6 jit_solution(14169711380635420403)
XLA Ops:
  7.2 0.0 all-gather.3.cloned.1.call-start
  7.2 0.7 all-gather.3.cloned.1.call-update
  7.9 0.0 reduce-scatter.2.cloned.1.call-start
  7.9 157.1 %all-gather.3.cloned.1.call-done = bf16[1024,6144]{1,0:T(8,128)(2,1)} async-done(((bf16[64,6144]{1,0:T(8,128)(2,1)}), bf16[1024,6144]{1,0:T(8,128)(2,1)}) %all-gather.3.cloned.1.call-update) | async-done | bytes 12582928 | tf_op jit(solution)/shard_map/all_gather | solution.py:18
  165.0 31.6 %fusion.11 = f32[256,6144]{1,0:T(8,128)} fusion(bf16[6144,6144]{1,0:T(8,128)(2,1)} %param.4, bf16[1024,6144]{1,0:T(8,128)(2,1)} %all-gather.3.cloned.1.call-done, s32[]{:T(128)S(6)} %select_n.6), kind=kOutput, calls=%fused_computation.17 | convolution fusion | flops 19327352832 | bytes 84934656 | tf_op jit(solution)/shard_map/dot_general | solution.py:21
  196.6 0.0 copy-start
  196.6 0.0 reduce-scatter.2.cloned.1.call-update
  196.6 0.0 all-gather.5.cloned.1.call-start
  196.7 12.3 %reduce-scatter.2.cloned.1.call-done = f32[128,6144]{1,0:T(8,128)} async-done(((f32[256,6144]{1,0:T(8,128)}), f32[128,6144]{1,0:T(8,128)}) %reduce-scatter.2.cloned.1.call-update) | async-done | bytes 3145744 | tf_op jit(solution)/shard_map/reduce_scatter | solution.py:22
  209.0 0.0 copy-done
  209.0 4.9 %fusion.2 = (bf16[128,6144]{1,0:T(8,128)(2,1)}, bf16[128,6144]{1,0:T(8,128)(2,1)}) fusion(bf16[128,6144]{1,0:T(8,128)(2,1)S(1)} %copy-done, f32[128,6144]{1,0:T(8,128)} %reduce-scatter.2.cloned.1.call-done), kind=kLoop, calls=%fused_computation.7 | loop fusion | flops 18087936 | bytes 7864320 | tf_op jit(solution)/shard_map/convert_element_type | solution.py:25
  213.9 0.0 all-gather.5.cloned.1.call-update
  214.0 74.2 %all-gather.5.cloned.1.call-done = bf16[1024,6144]{1,0:T(8,128)(2,1)} async-done(((bf16[128,6144]{1,0:T(8,128)(2,1)}), bf16[1024,6144]{1,0:T(8,128)(2,1)}) %all-gather.5.cloned.1.call-update) | async-done | bytes 12582928 | tf_op jit(solution)/shard_map/all_gather | solution.py:29
  288.1 27.9 %convolution_convert_fusion = bf16[1536,6144]{1,0:T(8,128)(2,1)} fusion(bf16[1024,6144]{1,0:T(8,128)(2,1)} %all-gather.5.cloned.1.call-done, bf16[1024,6144]{1,0:T(8,128)(2,1)} %all-gather.3.cloned.1.call-done, s32[]{:T(128)S(6)} %select_n.7), kind=kOutput, calls=%fused_computation | convolution fusion | flops 19336790016 | bytes 34603012 | tf_op jit(solution)/shard_map/dot_general | solution.py:12
Async XLA Ops:
  7.2 157.8 %all-gather.3.cloned.1.call-start = ((), (), s32[]{:S(2)}) async-start(), calls=%async_computation.1 | async-start | bytes 13369344 | tf_op jit(solution)/shard_map/all_gather | solution.py:18
  7.9 201.1 %reduce-scatter.2.cloned.1.call-start = ((), (), s32[]{:S(2)}) async-start(), calls=%async_computation.2 | async-start | bytes 9437184 | tf_op jit(solution)/shard_map/reduce_scatter | solution.py:22
  196.6 12.4 %copy-start = (bf16[128,6144]{1,0:T(8,128)(2,1)S(1)}, bf16[128,6144]{1,0:T(8,128)(2,1)}, u32[]{:S(2)}) copy-start(bf16[128,6144]{1,0:T(8,128)(2,1)} %param.5) | copy-start | bytes 4718596
  196.6 91.5 %all-gather.5.cloned.1.call-start = ((), (), s32[]{:S(2)}) async-start(), calls=%async_computation.3 | async-start | bytes 14155776 | tf_op jit(solution)/shard_map/all_gather | solution.py:29
Sparse Core Ops, SparseCore 0:
  10.8 154.1 all-gather.2
  196.8 12.2 reduce-scatter.1
  214.1 73.9 all-gather.4
where the time goes:
time: 323 us
  waiting for transfers between devices  244 us (76%)
  matrix products  59.5 us (18%)
  between operations  13.8 us (4%)
  other arithmetic  4.9 us (2%)
    all_gather x1, waiting for transfers between devices, local(): all_rows = lax.all_gather(tokens, ('dp', 'depth'), axis=0, tiled=True)  157 us
    all_gather x1, waiting for transfers between devices, local(): lax.all_gather(grad_pre, ('dp', 'grid'), axis=0, tiled=True)  74.2 us
    dot_general x1, matrix products, local(): partial_pre = jnp.dot(own_rows, weight, preferred_element_type=jnp.float32)  31.6 us
    dot_general x1, matrix products, transposed_product(): lax.dot_general(left, right, (((0,), (0,)), ((), ())), preferred_element_...  27.9 us
    reduce_scatter x1, waiting for transfers between devices, local(): lax.psum_scatter(partial_pre, 'grid', scatter_dimension=0, tiled=True)  12.3 us
  transfers between devices with their start and end apart: 3, of which 3 were waited for; matrix products, arithmetic and copies ran while one was open for 0% of the time, Pallas kernels for 0%

commit v1 on v0

v1 whole, which is shorter than its diff:
```python
import functools

import jax
import jax.numpy as jnp
from jax import lax
from jax.experimental import pallas as pl
from jax.experimental.pallas import tpu as pltpu
from jax.sharding import PartitionSpec as P

F32, BF16 = jnp.float32, jnp.bfloat16
CHUNKS = 4
LIMIT = 60 << 20


def gelu_tanh(values):
    return jax.nn.gelu(values, approximate=True)


def swap(values, axis, bits):
    return lax.ppermute(values, axis, [(i, i ^ bits) for i in range(lax.axis_size(axis))])


def divisor(size, most):
    return next(n for n in range(min(size, most), 0, -1) if size % n == 0 and (n % 128 == 0 or n == size))


def forward_kernel(rows, half, where_ref, x0, e1, o1, e2, o2, e3, w_ref, *rest):
    *outs, lines, total, sems = rest
    n, k = pl.program_id(0), pl.program_id(1)
    depth, side = where_ref[1], where_ref[2]
    low = depth < 2
    end = (depth == 0) | (depth == 3)
    third, fourth = jnp.where(low, 2, 1), jnp.where(low, 3, 0)

    def put(source, place, slot):
        return pltpu.make_async_copy(source, lines.at[pl.ds(pl.multiple_of(place * rows, rows), rows), :], sems.at[slot])

    @pl.when((n == 0) & (k == 0))
    def _():
        put(x0, depth, 0).start()
        put(e1, depth ^ 1, 1).start()

        @pl.when(end)
        def _():
            put(e2, third, 2).start()
            put(e3, fourth, 3).start()

        @pl.when(jnp.logical_not(end))
        def _():
            put(o1, third, 2).start()
            put(o2, fourth, 3).start()

        put(x0, depth, 0).wait()
        put(e1, depth ^ 1, 1).wait()
        put(e2, third, 2).wait()
        put(e3, fourth, 3).wait()

    bk = w_ref.shape[0]
    part = jnp.dot(lines[:, pl.ds(pl.multiple_of(k * bk, bk), bk)], w_ref[...], preferred_element_type=F32)
    last = pl.num_programs(1) - 1

    @pl.when(k == 0)
    def _():
        total[...] = part

    @pl.when(k > 0)
    def _():
        total[...] += part

    @pl.when(k == last)
    def _():
        if len(outs) == 1:
            outs[0][...] = total[...]
            return
        keep, send = outs

        @pl.when(side == 0)
        def _():
            keep[...] = total[:half, :]
            send[...] = total[half:, :].astype(BF16)

        @pl.when(side != 0)
        def _():
            keep[...] = total[half:, :]
            send[...] = total[:half, :].astype(BF16)


def forward(where, pieces, weight, chunk, width, pair):
    rows, feats = pieces[0].shape
    every = 4 * rows
    half = every // 2
    bn, bk = divisor(width, 768), divisor(feats, 1536)
    if pair:
        outs = [jax.ShapeDtypeStruct((half, width), F32), jax.ShapeDtypeStruct((half, width), BF16)]
    else:
        outs = [jax.ShapeDtypeStruct((every, width), F32)]
    first = chunk * (width // bn)
    return pl.pallas_call(
        functools.partial(forward_kernel, rows, half),
        grid_spec=pltpu.PrefetchScalarGridSpec(
            num_scalar_prefetch=1,
            grid=(width // bn, feats // bk),
            in_specs=[pl.BlockSpec(memory_space=pl.ANY)] * 6 + [pl.BlockSpec((bk, bn), lambda n, k, s: (k, first + n))],
            out_specs=[pl.BlockSpec((o.shape[0], bn), lambda n, k, s: (0, n)) for o in outs],
            scratch_shapes=[
                pltpu.VMEM((every, feats), BF16),
                pltpu.VMEM((every, bn), F32),
                pltpu.SemaphoreType.DMA((4,)),
            ],
        ),
        out_shape=outs,
        compiler_params=pltpu.CompilerParams(vmem_limit_bytes=LIMIT),
        cost_estimate=pl.CostEstimate(
            flops=2 * every * feats * width, bytes_accessed=2 * feats * width + 2 * every * feats, transcendentals=0
        ),
        name="fwd%d" % chunk,
    )(where, *pieces, weight)


def grad_kernel(chunk, rows, part, spots, pairs, steps, where_ref, *refs):
    count = 16 + len(spots)
    tokens, grads = refs[:16], refs[16:count]
    out, left, right, made, left_sems, right_sems, out_sems = refs[-7:]
    dp, depth, side = where_ref[0], where_ref[1], where_ref[2]
    low = depth < 2
    places = (depth, depth ^ 1, jnp.where(low, 2, 1), jnp.where(low, 3, 0))
    bn = made.shape[2]
    width = right.shape[1]

    loads = []
    for s in range(4):
        for r in range(4):
            at = pl.multiple_of(((dp ^ s) * 4 + places[r]) * rows, rows)
            loads.append(pltpu.make_async_copy(tokens[4 * s + r], left.at[pl.ds(at, rows), :], left_sems.at[4 * s + r]))
    feeds = []
    for n in range(steps):
        feeds.append([])
        for i, (s, other) in enumerate(spots):
            at = pl.multiple_of(((dp ^ s) * pairs + (jnp.abs(other - side) if pairs == 2 else 0)) * part, part)
            feeds[n].append(
                pltpu.make_async_copy(
                    grads[i].at[:, pl.ds(n * bn, bn)],
                    right.at[pl.ds(at, part), pl.ds(n * bn, bn)],
                    right_sems.at[n * len(spots) + i],
                )
            )
    for copy in loads:
        copy.start()
    for step in feeds:
        for copy in step:
            copy.start()
    for copy in loads:
        copy.wait()
    stores = []
    for n in range(steps):
        for copy in feeds[n]:
            copy.wait()
        if n >= 2:
            stores[n - 2].wait()
        made[n % 2] = lax.dot_general(
            left[...], right[:, n * bn : (n + 1) * bn], (((0,), (0,)), ((), ())), preferred_element_type=F32
        ).astype(BF16)
        stores.append(
            pltpu.make_async_copy(made.at[n % 2], out.at[:, pl.ds(chunk * width + n * bn, bn)], out_sems.at[n % 2])
        )
        stores[n].start()
    for copy in stores[-2:]:
        copy.wait()


def weight_grad_block(where, tokens, grads, spots, so_far, chunk, hidden_units, pairs):
    rows, sub = tokens[0].shape
    part, width = grads[0].shape
    every = 16 * rows
    bn = divisor(width, 512)
    steps = width // bn
    given = [] if so_far is None else [so_far]
    return pl.pallas_call(
        functools.partial(grad_kernel, chunk, rows, part, spots, pairs, steps),
        in_specs=[pl.BlockSpec(memory_space=pltpu.SMEM)]
        + [pl.BlockSpec(memory_space=pl.ANY)] * (16 + len(grads) + len(given)),
        out_specs=pl.BlockSpec(memory_space=pl.ANY),
        out_shape=jax.ShapeDtypeStruct((sub, hidden_units), BF16),
        scratch_shapes=[
            pltpu.VMEM((every, sub), BF16),
            pltpu.VMEM((every, width), BF16),
            pltpu.VMEM((2, sub, bn), BF16),
            pltpu.SemaphoreType.DMA((16,)),
            pltpu.SemaphoreType.DMA((steps * len(grads),)),
            pltpu.SemaphoreType.DMA((2,)),
        ],
        input_output_aliases={17 + len(grads): 0} if given else {},
        compiler_params=pltpu.CompilerParams(vmem_limit_bytes=LIMIT),
        cost_estimate=pl.CostEstimate(
            flops=2 * every * sub * width,
            bytes_accessed=2 * (every * sub + every * width + sub * width),
            transcendentals=0,
        ),
        name="bwd%d" % chunk,
    )(where, *tokens, *grads, *given)


def local(tokens, weight, cotangent):
    pair = lax.axis_size("grid") == 2
    dp, depth, side = (lax.axis_index(a) for a in ("dp", "depth", "grid"))
    where = jnp.stack([dp, depth, side]).astype(jnp.int32)
    hidden_units = weight.shape[1]
    sub = tokens.shape[1] // 4
    width = hidden_units // CHUNKS

    e1 = swap(tokens, "depth", 1)
    o1 = lax.ppermute(tokens, "depth", [(1, 2), (2, 1)])
    e2 = lax.ppermute(o1, "depth", [(1, 0), (2, 3)])
    o2 = lax.ppermute(e1, "depth", [(1, 2), (2, 1)])
    e3 = lax.ppermute(o2, "depth", [(1, 0), (2, 3)])
    end = (depth == 0) | (depth == 3)
    blocks = (tokens, e1, jnp.where(end, e2, o1), jnp.where(end, e3, o2))

    def columns(block, s):
        cut = lax.dynamic_slice_in_dim(block, (dp ^ s) * sub, sub, 1)
        return swap(cut, "dp", s) if s else cut

    lefts = [[columns(b, s) for b in blocks] for s in range(4)]
    lefts = [b for group in lefts for b in group]

    hidden, grad = [], None
    for j in range(CHUNKS):
        made = forward(where, (tokens, e1, o1, e2, o2, e3), weight, j, width, pair)
        if pair:
            preact = made[0] + swap(made[1], "grid", 1).astype(F32)
        else:
            preact = lax.psum_scatter(made[0], "grid", scatter_dimension=0, tiled=True)
        activated, pullback = jax.vjp(gelu_tanh, preact)
        hidden.append(activated.astype(BF16))
        cot = lax.slice_in_dim(cotangent, j * width, (j + 1) * width, axis=1)
        own = pullback(cot.astype(F32))[0].astype(BF16)
        if not pair:
            own = lax.all_gather(own, "grid", axis=0, tiled=True)
        a, b = swap(own, "dp", 1), swap(own, "dp", 2)
        c = swap(b, "dp", 1) if j % 2 == 0 else swap(a, "dp", 2)
        grads, spots = [own, a, b, c], [(0, 0), (1, 0), (2, 0), (3, 0)]
        if pair:
            grads += [swap(v, "grid", 1) for v in grads]
            spots += [(s, 1) for s, _ in spots]
        grad = weight_grad_block(where, lefts, grads, tuple(spots), grad, j, hidden_units, 2 if pair else 1)
    return (jnp.concatenate(hidden, axis=1), grad)


def solution(mesh):
    assert mesh.shape["dp"] == 4 and mesh.shape["depth"] == 4
    return jax.shard_map(
        local,
        mesh=mesh,
        in_specs=(P(("dp", "depth"), "grid"), P("grid", "depth"), P(("dp", "grid"), "depth")),
        out_specs=(P(("dp", "grid"), "depth"), P(("grid", "dp"), "depth")),
        check_vma=False,
    )
```

time: 323 us -> 259 us (0.80)
  waiting for transfers between devices: 244 us -> 97.8 us
  Pallas kernels: 0 us -> 104 us
  matrix products: 59.5 us -> 0 us
  starting transfers between devices: 0.12 us -> 40.8 us
  between operations: 13.8 us -> 1.5 us
  local copies, waits for them, and re-layouts: 0.01 us -> 8.15 us
    all_gather x2 -> x0, waiting for transfers between devices: 231 us -> none  [the longest x1 157 us: local(): all_rows = lax.all_gather(tokens, ('dp', 'depth'), axis=0, tiled=True)]
    pallas_call x0 -> x8, Pallas kernels: none -> 104 us  [the longest x4 61.8 us: forward(): pl.pallas_call(functools.partial(forward_kernel, rows, half), grid_spec=p...]
    ppermute x0 -> x49, waiting for transfers between devices: none -> 97.8 us  [the longest x45 68.6 us: swap(): lax.ppermute(values, axis, [(i, i ^ bits) for i in range(lax.axis_size(ax...]
    dot_general x2 -> x0, matrix products: 59.5 us -> none  [the longest x1 31.6 us: local(): partial_pre = jnp.dot(own_rows, weight, preferred_element_type=jnp.float32)]
    ppermute x0 -> x49, starting transfers between devices: none -> 40.8 us  [the longest x45 36.9 us: swap(): lax.ppermute(values, axis, [(i, i ^ bits) for i in range(lax.axis_size(ax...]
    reduce_scatter x1 -> x0, waiting for transfers between devices: 12.3 us -> none  [local(): lax.psum_scatter(partial_pre, 'grid', scatter_dimension=0, tiled=True)]
    dynamic_slice x0 -> x4, local copies, waits for them, and re-layouts: none -> 4.72 us  [columns(): cut = lax.dynamic_slice_in_dim(block, (dp ^ s) * sub, sub, 1)]
    unnamed x2 -> x96, local copies, waits for them, and re-layouts: 0.01 us -> 3.42 us
  transfers between devices with their start and end apart: 3 -> 49, of which waited for: 3 -> 12; matrix products, arithmetic and copies ran while one was open for 0% -> 4% of each run, Pallas kernels for 0% -> 36%
where the time goes in v1:
time: 259 us; the launch traced here: 258 us
  Pallas kernels  104 us (40%)
  waiting for transfers between devices  97.8 us (38%)
  starting transfers between devices  40.8 us (16%)
  local copies, waits for them, and re-layouts  8.15 us (3%)
  other arithmetic  5.91 us (2%)
    ppermute x45, waiting for transfers between devices, swap(): lax.ppermute(values, axis, [(i, i ^ bits) for i in range(lax.axis_size(ax...  68.6 us
    pallas_call x4, Pallas kernels, forward(): pl.pallas_call(functools.partial(forward_kernel, rows, half), grid_spec=p...  61.8 us
    pallas_call x4, Pallas kernels, weight_grad_block(): pl.pallas_call(functools.partial(grad_kernel, chunk, rows, part, spots, p...  42.4 us
    ppermute x45, starting transfers between devices, swap(): lax.ppermute(values, axis, [(i, i ^ bits) for i in range(lax.axis_size(ax...  36.9 us
    ppermute x1, waiting for transfers between devices, local(): e3 = lax.ppermute(o2, 'depth', [(1, 0), (2, 3)])  17.1 us
    ppermute x1, waiting for transfers between devices, local(): e2 = lax.ppermute(o1, 'depth', [(1, 0), (2, 3)])  12.1 us
  transfers between devices with their start and end apart: 49, of which 12 were waited for; matrix products, arithmetic and copies ran while one was open for 4% of the time, Pallas kernels for 36%

profile of v1, /device:TPU:0, one launch (start us, length us, event | category | flops | bytes accessed | tf_op | source)
XLA Modules:
  0.0 258.3 jit_solution(13878693543640139929)
XLA Ops:
  0.6 3.1 %collective-permute-start = (bf16[64,6144]{1,0:T(8,128)(2,1)}, bf16[64,6144]{1,0:T(8,128)(2,1)S(1)}, u32[]{:S(2)}, u32[]{:S(2)}) collective-permute-start(bf16[64,6144]{1,0:T(8,128)(2,1)} %x0.7), channel_id=1, source_target_pairs={{0,2},{2,0},{4,6},{6,4},{1,3},{3,1},{5,7},{7,5},{8,10},{10,8},{12,... | collective-permute-start | bytes 2359304 | tf_op jit(solution)/shard_map/ppermute | solution.py:20
  4.5 17.0 %collective-permute-done.e1 = bf16[64,6144]{1,0:T(8,128)(2,1)S(1)} collective-permute-done((bf16[64,6144]{1,0:T(8,128)(2,1)}, bf16[64,6144]{1,0:T(8,128)(2,1)S(1)}, u32[]{:S(2)}, u32[]{:S(2)}) %collective-permute-start) | collective-permute-done | bytes 786464 | tf_op jit(solution)/shard_map/ppermute | solution.py:20
  23.6 2.1 constant_dynamic-slice_fusion.3
  25.7 1.7 collective-permute-start.13
  30.7 1.7 collective-permute-start.10
  32.4 12.1 %collective-permute-done.2.e2 = bf16[64,6144]{1,0:T(8,128)(2,1)S(1)} collective-permute-done((bf16[64,6144]{1,0:T(8,128)(2,1)S(1)}, bf16[64,6144]{1,0:T(8,128)(2,1)S(1)}, u32[]{:S(2)}, u32[]{:S(2)}) %collective-permute-start.2) | collective-permute-done | bytes 786464 | tf_op jit(solution)/shard_map/ppermute | solution.py:213
  46.8 17.1 %collective-permute-done.4.e3 = bf16[64,6144]{1,0:T(8,128)(2,1)S(1)} collective-permute-done((bf16[64,6144]{1,0:T(8,128)(2,1)S(1)}, bf16[64,6144]{1,0:T(8,128)(2,1)S(1)}, u32[]{:S(2)}, u32[]{:S(2)}) %collective-permute-start.4) | collective-permute-done | bytes 786464 | tf_op jit(solution)/shard_map/ppermute | solution.py:215
  64.8 1.5 collective-permute-start.14
  66.3 15.4 %fwd1.1 = (f32[128,1536]{1,0:T(8,128)}, bf16[128,1536]{1,0:T(8,128)(2,1)}) custom-call(s32[3]{0:T(128)} %pad_add_fusion.where_ref, bf16[64,6144]{1,0:T(8,128)(2,1)} %x0.7, bf16[64,6144]{1,0:T(8,128)(2,1)} %copy-done.2, bf16[64,6144]{1,0:T(8,128)(2,1)} %copy-done.3, bf16[64,6144]{1,0:T(8,128)(2,1)} %copy-done.4, bf16[64,6144]{1,0:T(8,128)(2,1)} %copy-done, ...), custom_call_target="tpu_custom_call" | custom-call | flops 4831838208 | bytes 22020096 | tf_op jit(solution)/shard_map/fwd1/pallas_call | solution.py:98
  81.7 15.3 %fwd3.1 = (f32[128,1536]{1,0:T(8,128)}, bf16[128,1536]{1,0:T(8,128)(2,1)}) custom-call(s32[3]{0:T(128)} %pad_add_fusion.where_ref, bf16[64,6144]{1,0:T(8,128)(2,1)} %x0.7, bf16[64,6144]{1,0:T(8,128)(2,1)} %copy-done.2, bf16[64,6144]{1,0:T(8,128)(2,1)} %copy-done.3, bf16[64,6144]{1,0:T(8,128)(2,1)} %copy-done.4, bf16[64,6144]{1,0:T(8,128)(2,1)} %copy-done, ...), custom_call_target="tpu_custom_call" | custom-call | flops 4831838208 | bytes 22020096 | tf_op jit(solution)/shard_map/fwd3/pallas_call | solution.py:98
  97.1 15.5 %fwd2.1 = (f32[128,1536]{1,0:T(8,128)}, bf16[128,1536]{1,0:T(8,128)(2,1)}) custom-call(s32[3]{0:T(128)} %pad_add_fusion.where_ref, bf16[64,6144]{1,0:T(8,128)(2,1)} %x0.7, bf16[64,6144]{1,0:T(8,128)(2,1)} %copy-done.2, bf16[64,6144]{1,0:T(8,128)(2,1)} %copy-done.3, bf16[64,6144]{1,0:T(8,128)(2,1)} %copy-done.4, bf16[64,6144]{1,0:T(8,128)(2,1)} %copy-done, ...), custom_call_target="tpu_custom_call" | custom-call | flops 4831838208 | bytes 22020096 | tf_op jit(solution)/shard_map/fwd2/pallas_call | solution.py:98
  112.6 15.5 %fwd0.1 = (f32[128,1536]{1,0:T(8,128)}, bf16[128,1536]{1,0:T(8,128)(2,1)}) custom-call(s32[3]{0:T(128)} %pad_add_fusion.where_ref, bf16[64,6144]{1,0:T(8,128)(2,1)} %x0.7, bf16[64,6144]{1,0:T(8,128)(2,1)} %copy-done.2, bf16[64,6144]{1,0:T(8,128)(2,1)} %copy-done.3, bf16[64,6144]{1,0:T(8,128)(2,1)} %copy-done.4, bf16[64,6144]{1,0:T(8,128)(2,1)} %copy-done, ...), custom_call_target="tpu_custom_call" | custom-call | flops 4831838208 | bytes 22020096 | tf_op jit(solution)/shard_map/fwd0/pallas_call | solution.py:98
  129.4 1.5 collective-permute-start.18
  131.6 5.6 %collective-permute-done.18.refs_13_ = bf16[64,1536]{1,0:T(8,128)(2,1)S(1)} collective-permute-done((bf16[64,1536]{1,0:T(8,128)(2,1)S(1)}, bf16[64,1536]{1,0:T(8,128)(2,1)S(1)}, u32[]{:S(2)}, u32[]{:S(2)}) %collective-permute-start.18) | collective-permute-done | bytes 196640 | tf_op jit(solution)/shard_map/ppermute | solution.py:20
  142.8 3.8 %fusion.17 = (bf16[128,1536]{1,0:T(8,128)(2,1)S(1)}, bf16[128,1536]{1,0:T(8,128)(2,1)S(1)}, bf16[128,1536]{1,0:T(8,128)(2,1)S(1)}, bf16[128,1536]{1,0:T(8,128)(2...) fusion(f32[128,1536]{1,0:T(8,128)} %get-tuple-element.10, ...), kind=kLoop, calls=%fused_computation.34 | loop fusion | flops 19660800 | bytes 9437184 | tf_op jit(solution)/shard_map/convert_element_type | solution.py:236
  146.8 1.6 collective-permute-start.43
  148.3 2.2 collective-permute-done.15.refs_10_
  151.4 2.3 collective-permute-done.12.refs_7_
  155.7 17.3 %collective-permute-done.20.refs_15_ = bf16[64,1536]{1,0:T(8,128)(2,1)S(1)} collective-permute-done((bf16[64,1536]{1,0:T(8,128)(2,1)S(1)}, bf16[64,1536]{1,0:T(8,128)(2,1)S(1)}, u32[]{:S(2)}, u32[]{:S(2)}) %collective-permute-start.20) | collective-permute-done | bytes 196640 | tf_op jit(solution)/shard_map/ppermute | solution.py:20
  173.0 1.5 collective-permute-start.36
  177.1 7.9 %collective-permute-done.36.refs_18_ = bf16[128,1536]{1,0:T(8,128)(2,1)} collective-permute-done((bf16[128,1536]{1,0:T(8,128)(2,1)S(1)}, bf16[128,1536]{1,0:T(8,128)(2,1)}, u32[]{:S(2)}, u32[]{:S(2)}) %collective-permute-start.36) | collective-permute-done | bytes 393248 | tf_op jit(solution)/shard_map/ppermute | solution.py:20
  185.6 4.3 %collective-permute-done.29.refs_18_ = bf16[128,1536]{1,0:T(8,128)(2,1)S(1)} collective-permute-done((bf16[128,1536]{1,0:T(8,128)(2,1)S(1)}, bf16[128,1536]{1,0:T(8,128)(2,1)S(1)}, u32[]{:S(2)}, u32[]{:S(2)}) %collective-permute-start.29) | collective-permute-done | bytes 393248 | tf_op jit(solution)/shard_map/ppermute | solution.py:20
  189.9 1.8 collective-permute-start.37
  191.7 3.0 %collective-permute-done.44.refs_19_ = bf16[128,1536]{1,0:T(8,128)(2,1)S(1)} collective-permute-done((bf16[128,1536]{1,0:T(8,128)(2,1)S(1)}, bf16[128,1536]{1,0:T(8,128)(2,1)S(1)}, u32[]{:S(2)}, u32[]{:S(2)}) %collective-permute-start.44) | collective-permute-done | bytes 393248 | tf_op jit(solution)/shard_map/ppermute | solution.py:20
  198.0 3.8 %collective-permute-done.37.refs_19_ = bf16[128,1536]{1,0:T(8,128)(2,1)} collective-permute-done((bf16[128,1536]{1,0:T(8,128)(2,1)}, bf16[128,1536]{1,0:T(8,128)(2,1)}, u32[]{:S(2)}, u32[]{:S(2)}) %collective-permute-start.37) | collective-permute-done | bytes 393248 | tf_op jit(solution)/shard_map/ppermute | solution.py:20
  201.8 2.4 collective-permute-start.30
  205.0 10.6 %bwd0.1.refs_24_ = bf16[1536,6144]{1,0:T(8,128)(2,1)} custom-call(s32[3]{0:T(128)} %pad_add_fusion.where_ref, bf16[64,1536]{1,0:T(8,128)(2,1)} %get-tuple-element.40.refs_0_, bf16[64,1536]{1,0:T(8,128)(2,1)} %get-tuple-element.37.refs_1_, bf16[64,1536]{1,0:T(8,128)(2,1)} %get-tuple-element.33.refs_2_, bf16[64,1536]{1,0:T(8,128)(2,1)} %get-tuple-element.29.refs_3_, ...), custom_call_target="tpu_custom_call" | custom-call | flops 4831838208 | bytes 11010048 | tf_op jit(solution)/shard_map/bwd0/pallas_call | solution.py:178
  215.7 1.6 collective-permute-start.22
  218.3 10.6 %bwd1.1.refs_24_ = bf16[1536,6144]{1,0:T(8,128)(2,1)} custom-call(s32[3]{0:T(128)} %pad_add_fusion.where_ref, bf16[64,1536]{1,0:T(8,128)(2,1)} %get-tuple-element.40.refs_0_, bf16[64,1536]{1,0:T(8,128)(2,1)} %get-tuple-element.37.refs_1_, bf16[64,1536]{1,0:T(8,128)(2,1)} %get-tuple-element.33.refs_2_, ...), custom_call_target="tpu_custom_call", output_to_operand_aliasing={{}: (25, {})} | custom-call | flops 4831838208 | bytes 11010048 | tf_op jit(solution)/shard_map/bwd1/pallas_call | solution.py:178
  230.1 5.0 %collective-permute-done.23.refs_19_ = bf16[128,1536]{1,0:T(8,128)(2,1)S(1)} collective-permute-done((bf16[128,1536]{1,0:T(8,128)(2,1)S(1)}, bf16[128,1536]{1,0:T(8,128)(2,1)S(1)}, u32[]{:S(2)}, u32[]{:S(2)}) %collective-permute-start.23) | collective-permute-done | bytes 393248 | tf_op jit(solution)/shard_map/ppermute | solution.py:20
  235.1 10.6 %bwd2.1.refs_24_ = bf16[1536,6144]{1,0:T(8,128)(2,1)} custom-call(s32[3]{0:T(128)} %pad_add_fusion.where_ref, bf16[64,1536]{1,0:T(8,128)(2,1)} %get-tuple-element.40.refs_0_, bf16[64,1536]{1,0:T(8,128)(2,1)} %get-tuple-element.37.refs_1_, bf16[64,1536]{1,0:T(8,128)(2,1)} %get-tuple-element.33.refs_2_, ...), custom_call_target="tpu_custom_call", output_to_operand_aliasing={{}: (25, {})} | custom-call | flops 4831838208 | bytes 11010048 | tf_op jit(solution)/shard_map/bwd2/pallas_call | solution.py:178
  247.5 10.6 %bwd3.1 = bf16[1536,6144]{1,0:T(8,128)(2,1)} custom-call(s32[3]{0:T(128)} %pad_add_fusion.where_ref, bf16[64,1536]{1,0:T(8,128)(2,1)} %get-tuple-element.40.refs_0_, bf16[64,1536]{1,0:T(8,128)(2,1)} %get-tuple-element.37.refs_1_, bf16[64,1536]{1,0:T(8,128)(2,1)} %get-tuple-element.33.refs_2_, ...), custom_call_target="tpu_custom_call", output_to_operand_aliasing={{}: (25, {})} | custom-call | flops 4831838208 | bytes 11010048 | tf_op jit(solution)/shard_map/bwd3/pallas_call | solution.py:178
  (179 shorter events, 30.6 us)
Async XLA Ops:
  0.6 20.9 %collective-permute-start = (bf16[64,6144]{1,0:T(8,128)(2,1)}, bf16[64,6144]{1,0:T(8,128)(2,1)S(1)}, u32[]{:S(2)}, u32[]{:S(2)}) collective-permute-start(bf16[64,6144]{1,0:T(8,128)(2,1)} %x0.7), channel_id=1, source_target_pairs={{0,2},{2,0},{4,6},{6,4},{1,3},{3,1},{5,7},{7,5},{8,10},{10,8},{12,... | collective-permute-start | bytes 2359304 | tf_op jit(solution)/shard_map/ppermute | solution.py:20
  3.7 18.5 %collective-permute-start.1 = (bf16[64,6144]{1,0:T(8,128)(2,1)}, bf16[64,6144]{1,0:T(8,128)(2,1)S(1)}, u32[]{:S(2)}, u32[]{:S(2)}) collective-permute-start(bf16[64,6144]{1,0:T(8,128)(2,1)} %x0.7), channel_id=1, source_target_pairs={{2,4},{4,2},{3,5},{5,3},{10,12},{12,10},{11,13},{13,11},{18,20},{2... | collective-permute-start | bytes 2359304 | tf_op jit(solution)/shard_map/ppermute | solution.py:212
  22.2 22.2 %collective-permute-start.2 = (bf16[64,6144]{1,0:T(8,128)(2,1)S(1)}, bf16[64,6144]{1,0:T(8,128)(2,1)S(1)}, u32[]{:S(2)}, u32[]{:S(2)}) collective-permute-start(bf16[64,6144]{1,0:T(8,128)(2,1)S(1)} %collective-permute-done.1.o1), channel_id=1, source_target_pairs={{2,0},{4,6},{3,1},{5,7},{10,8},{12,14},{11,9},{13,15},{18,16},{20,... | collective-permute-start | bytes 2359304 | tf_op jit(solution)/shard_map/ppermute | solution.py:213
  25.7 102.5 %collective-permute-start.13 = (bf16[64,1536]{1,0:T(8,128)(2,1)}, bf16[64,1536]{1,0:T(8,128)(2,1)S(1)}, u32[]{:S(2)}, u32[]{:S(2)}) collective-permute-start(bf16[64,1536]{1,0:T(8,128)(2,1)} %get-tuple-element.41), channel_id=1, source_target_pairs={{0,16},{8,24},{16,0},{24,8},{1,17},{9,25},{17,1},{25,9},{2,18},{10... | collective-permute-start | bytes 589832 | tf_op jit(solution)/shard_map/ppermute | solution.py:20
  27.4 100.9 %collective-permute-start.17 = (bf16[64,1536]{1,0:T(8,128)(2,1)}, bf16[64,1536]{1,0:T(8,128)(2,1)S(1)}, u32[]{:S(2)}, u32[]{:S(2)}) collective-permute-start(bf16[64,1536]{1,0:T(8,128)(2,1)} %get-tuple-element.38), channel_id=1, source_target_pairs={{0,24},{8,16},{16,8},{24,0},{1,25},{9,17},{17,9},{25,1},{2,26},{10... | collective-permute-start | bytes 589832 | tf_op jit(solution)/shard_map/ppermute | solution.py:20
  28.8 100.0 %collective-permute-start.9 = (bf16[64,1536]{1,0:T(8,128)(2,1)}, bf16[64,1536]{1,0:T(8,128)(2,1)}, u32[]{:S(2)}, u32[]{:S(2)}) collective-permute-start(bf16[64,1536]{1,0:T(8,128)(2,1)} %get-tuple-element.39), channel_id=1, source_target_pairs={{0,8},{8,0},{16,24},{24,16},{1,9},{9,1},{17,25},{25,17},{2,10},{10... | collective-permute-start | bytes 589832 | tf_op jit(solution)/shard_map/ppermute | solution.py:20
  30.7 98.2 %collective-permute-start.10 = (bf16[64,1536]{1,0:T(8,128)(2,1)}, bf16[64,1536]{1,0:T(8,128)(2,1)}, u32[]{:S(2)}, u32[]{:S(2)}) collective-permute-start(bf16[64,1536]{1,0:T(8,128)(2,1)} %get-tuple-element.36), channel_id=1, source_target_pairs={{0,8},{8,0},{16,24},{24,16},{1,9},{9,1},{17,25},{25,17},{2,10},{10... | collective-permute-start | bytes 589832 | tf_op jit(solution)/shard_map/ppermute | solution.py:20
  44.4 19.5 %collective-permute-start.4 = (bf16[64,6144]{1,0:T(8,128)(2,1)S(1)}, bf16[64,6144]{1,0:T(8,128)(2,1)S(1)}, u32[]{:S(2)}, u32[]{:S(2)}) collective-permute-start(bf16[64,6144]{1,0:T(8,128)(2,1)S(1)} %collective-permute-done.3.o2), channel_id=1, source_target_pairs={{2,0},{4,6},{3,1},{5,7},{10,8},{12,14},{11,9},{13,15},{18,16},{20,... | collective-permute-start | bytes 2359304 | tf_op jit(solution)/shard_map/ppermute | solution.py:215
  64.8 64.6 %collective-permute-start.14 = (bf16[64,1536]{1,0:T(8,128)(2,1)}, bf16[64,1536]{1,0:T(8,128)(2,1)S(1)}, u32[]{:S(2)}, u32[]{:S(2)}) collective-permute-start(bf16[64,1536]{1,0:T(8,128)(2,1)} %get-tuple-element.35), channel_id=1, source_target_pairs={{0,16},{8,24},{16,0},{24,8},{1,17},{9,25},{17,1},{25,9},{2,18},{10... | collective-permute-start | bytes 589832 | tf_op jit(solution)/shard_map/ppermute | solution.py:20
  128.9 13.4 %collective-permute-start.5 = (bf16[128,1536]{1,0:T(8,128)(2,1)}, bf16[128,1536]{1,0:T(8,128)(2,1)S(1)}, u32[]{:S(2)}, u32[]{:S(2)}) collective-permute-start(bf16[128,1536]{1,0:T(8,128)(2,1)} %get-tuple-element.11), channel_id=1, source_target_pairs={{0,1},{1,0},{2,3},{3,2},{4,5},{5,4},{6,7},{7,6},{8,9},{9,8},{10,11... | collective-permute-start | bytes 1179656 | tf_op jit(solution)/shard_map/ppermute | solution.py:20
  140.8 12.9 %collective-permute-start.12 = (bf16[64,1536]{1,0:T(8,128)(2,1)S(1)}, bf16[64,1536]{1,0:T(8,128)(2,1)S(1)}, u32[]{:S(2)}, u32[]{:S(2)}) collective-permute-start(bf16[64,1536]{1,0:T(8,128)(2,1)S(1)} %get-tuple-element.28), channel_id=1, source_target_pairs={{0,8},{8,0},{16,24},{24,16},{1,9},{9,1},{17,25},{25,17},{2,10},{10... | collective-permute-start | bytes 589832 | tf_op jit(solution)/shard_map/ppermute | solution.py:20
  142.3 12.9 %collective-permute-start.16 = (bf16[64,1536]{1,0:T(8,128)(2,1)S(1)}, bf16[64,1536]{1,0:T(8,128)(2,1)S(1)}, u32[]{:S(2)}, u32[]{:S(2)}) collective-permute-start(bf16[64,1536]{1,0:T(8,128)(2,1)S(1)} %get-tuple-element.27), channel_id=1, source_target_pairs={{0,16},{8,24},{16,0},{24,8},{1,17},{9,25},{17,1},{25,9},{2,18},{10... | collective-permute-start | bytes 589832 | tf_op jit(solution)/shard_map/ppermute | solution.py:20
  146.8 27.7 %collective-permute-start.43 = (bf16[128,1536]{1,0:T(8,128)(2,1)S(1)}, bf16[128,1536]{1,0:T(8,128)(2,1)S(1)}, u32[]{:S(2)}, u32[]{:S(2)}) collective-permute-start(bf16[128,1536]{1,0:T(8,128)(2,1)S(1)} %get-tuple-element.18.refs_16_), channel_id=1, source_target_pairs={{0,16},{8,24},{16,0},{24,8},{1,17},{9,25},{17,1},{25,9},{2,18},{10... | collective-permute-start | bytes 1179656 | tf_op jit(solution)/shard_map/ppermute | solution.py:20
  150.6 23.9 %collective-permute-start.42 = (bf16[128,1536]{1,0:T(8,128)(2,1)S(1)}, bf16[128,1536]{1,0:T(8,128)(2,1)S(1)}, u32[]{:S(2)}, u32[]{:S(2)}) collective-permute-start(bf16[128,1536]{1,0:T(8,128)(2,1)S(1)} %get-tuple-element.18.refs_16_), channel_id=1, source_target_pairs={{0,8},{8,0},{16,24},{24,16},{1,9},{9,1},{17,25},{25,17},{2,10},{10... | collective-permute-start | bytes 1179656 | tf_op jit(solution)/shard_map/ppermute | solution.py:20
  151.4 23.7 %collective-permute-start.45 = (bf16[128,1536]{1,0:T(8,128)(2,1)S(1)}, bf16[128,1536]{1,0:T(8,128)(2,1)S(1)}, u32[]{:S(2)}, u32[]{:S(2)}) collective-permute-start(bf16[128,1536]{1,0:T(8,128)(2,1)S(1)} %get-tuple-element.18.refs_16_), channel_id=1, source_target_pairs={{0,1},{1,0},{2,3},{3,2},{4,5},{5,4},{6,7},{7,6},{8,9},{9,8},{10,11... | collective-permute-start | bytes 1179656 | tf_op jit(solution)/shard_map/ppermute | solution.py:20
  153.7 22.9 %collective-permute-start.35 = (bf16[128,1536]{1,0:T(8,128)(2,1)S(1)}, bf16[128,1536]{1,0:T(8,128)(2,1)}, u32[]{:S(2)}, u32[]{:S(2)}) collective-permute-start(bf16[128,1536]{1,0:T(8,128)(2,1)S(1)} %get-tuple-element.21.refs_16_), channel_id=1, source_target_pairs={{0,8},{8,0},{16,24},{24,16},{1,9},{9,1},{17,25},{25,17},{2,10},{10... | collective-permute-start | bytes 1179656 | tf_op jit(solution)/shard_map/ppermute | solution.py:20
  155.2 17.8 %collective-permute-start.20 = (bf16[64,1536]{1,0:T(8,128)(2,1)S(1)}, bf16[64,1536]{1,0:T(8,128)(2,1)S(1)}, u32[]{:S(2)}, u32[]{:S(2)}) collective-permute-start(bf16[64,1536]{1,0:T(8,128)(2,1)S(1)} %get-tuple-element.26), channel_id=1, source_target_pairs={{0,24},{8,16},{16,8},{24,0},{1,25},{9,17},{17,9},{25,1},{2,26},{10... | collective-permute-start | bytes 589832 | tf_op jit(solution)/shard_map/ppermute | solution.py:20
  174.5 15.3 %collective-permute-start.29 = (bf16[128,1536]{1,0:T(8,128)(2,1)S(1)}, bf16[128,1536]{1,0:T(8,128)(2,1)S(1)}, u32[]{:S(2)}, u32[]{:S(2)}) collective-permute-start(bf16[128,1536]{1,0:T(8,128)(2,1)S(1)} %get-tuple-element.19.refs_16_), channel_id=1, source_target_pairs={{0,16},{8,24},{16,0},{24,8},{1,17},{9,25},{17,1},{25,9},{2,18},{10... | collective-permute-start | bytes 1179656 | tf_op jit(solution)/shard_map/ppermute | solution.py:20
  175.1 14.8 %collective-permute-start.28 = (bf16[128,1536]{1,0:T(8,128)(2,1)S(1)}, bf16[128,1536]{1,0:T(8,128)(2,1)S(1)}, u32[]{:S(2)}, u32[]{:S(2)}) collective-permute-start(bf16[128,1536]{1,0:T(8,128)(2,1)S(1)} %get-tuple-element.19.refs_16_), channel_id=1, source_target_pairs={{0,8},{8,0},{16,24},{24,16},{1,9},{9,1},{17,25},{25,17},{2,10},{10... | collective-permute-start | bytes 1179656 | tf_op jit(solution)/shard_map/ppermute | solution.py:20
  176.6 18.1 %collective-permute-start.44 = (bf16[128,1536]{1,0:T(8,128)(2,1)S(1)}, bf16[128,1536]{1,0:T(8,128)(2,1)S(1)}, u32[]{:S(2)}, u32[]{:S(2)}) collective-permute-start(bf16[128,1536]{1,0:T(8,128)(2,1)S(1)} %collective-permute-done.43.refs_18_), channel_id=1, source_target_pairs={{0,8},{8,0},{16,24},{24,16},{1,9},{9,1},{17,25},{25,17},{2,10},{10... | collective-permute-start | bytes 1179656 | tf_op jit(solution)/shard_map/ppermute | solution.py:20
  185.1 12.7 %collective-permute-start.47 = (bf16[128,1536]{1,0:T(8,128)(2,1)S(1)}, bf16[128,1536]{1,0:T(8,128)(2,1)S(1)}, u32[]{:S(2)}, u32[]{:S(2)}) collective-permute-start(bf16[128,1536]{1,0:T(8,128)(2,1)S(1)} %collective-permute-done.43.refs_18_), channel_id=1, source_target_pairs={{0,1},{1,0},{2,3},{3,2},{4,5},{5,4},{6,7},{7,6},{8,9},{9,8},{10,11... | collective-permute-start | bytes 1179656 | tf_op jit(solution)/shard_map/ppermute | solution.py:20
  196.0 19.6 %collective-permute-start.21 = (bf16[128,1536]{1,0:T(8,128)(2,1)S(1)}, bf16[128,1536]{1,0:T(8,128)(2,1)S(1)}, u32[]{:S(2)}, u32[]{:S(2)}) collective-permute-start(bf16[128,1536]{1,0:T(8,128)(2,1)S(1)} %get-tuple-element.20.refs_16_), channel_id=1, source_target_pairs={{0,8},{8,0},{16,24},{24,16},{1,9},{9,1},{17,25},{25,17},{2,10},{10... | collective-permute-start | bytes 1179656 | tf_op jit(solution)/shard_map/ppermute | solution.py:20
  197.5 19.7 %collective-permute-start.39 = (bf16[128,1536]{1,0:T(8,128)(2,1)}, bf16[128,1536]{1,0:T(8,128)(2,1)}, u32[]{:S(2)}, u32[]{:S(2)}) collective-permute-start(bf16[128,1536]{1,0:T(8,128)(2,1)} %collective-permute-done.35.refs_17_), channel_id=1, source_target_pairs={{0,1},{1,0},{2,3},{3,2},{4,5},{5,4},{6,7},{7,6},{8,9},{9,8},{10,11... | collective-permute-start | bytes 1179656 | tf_op jit(solution)/shard_map/ppermute | solution.py:20
  197.8 19.5 %collective-permute-start.40 = (bf16[128,1536]{1,0:T(8,128)(2,1)}, bf16[128,1536]{1,0:T(8,128)(2,1)}, u32[]{:S(2)}, u32[]{:S(2)}) collective-permute-start(bf16[128,1536]{1,0:T(8,128)(2,1)} %collective-permute-done.36.refs_18_), channel_id=1, source_target_pairs={{0,1},{1,0},{2,3},{3,2},{4,5},{5,4},{6,7},{7,6},{8,9},{9,8},{10,11... | collective-permute-start | bytes 1179656 | tf_op jit(solution)/shard_map/ppermute | solution.py:20
  201.8 16.0 %collective-permute-start.30 = (bf16[128,1536]{1,0:T(8,128)(2,1)S(1)}, bf16[128,1536]{1,0:T(8,128)(2,1)}, u32[]{:S(2)}, u32[]{:S(2)}) collective-permute-start(bf16[128,1536]{1,0:T(8,128)(2,1)S(1)} %collective-permute-done.29.refs_18_), channel_id=1, source_target_pairs={{0,8},{8,0},{16,24},{24,16},{1,9},{9,1},{17,25},{25,17},{2,10},{10... | collective-permute-start | bytes 1179656 | tf_op jit(solution)/shard_map/ppermute | solution.py:20
  204.2 14.0 %collective-permute-start.41 = (bf16[128,1536]{1,0:T(8,128)(2,1)}, bf16[128,1536]{1,0:T(8,128)(2,1)}, u32[]{:S(2)}, u32[]{:S(2)}) collective-permute-start(bf16[128,1536]{1,0:T(8,128)(2,1)} %collective-permute-done.37.refs_19_), channel_id=1, source_target_pairs={{0,1},{1,0},{2,3},{3,2},{4,5},{5,4},{6,7},{7,6},{8,9},{9,8},{10,11... | collective-permute-start | bytes 1179656 | tf_op jit(solution)/shard_map/ppermute | solution.py:20
  215.7 13.2 %collective-permute-start.22 = (bf16[128,1536]{1,0:T(8,128)(2,1)S(1)}, bf16[128,1536]{1,0:T(8,128)(2,1)S(1)}, u32[]{:S(2)}, u32[]{:S(2)}) collective-permute-start(bf16[128,1536]{1,0:T(8,128)(2,1)S(1)} %get-tuple-element.20.refs_16_), channel_id=1, source_target_pairs={{0,16},{8,24},{16,0},{24,8},{1,17},{9,25},{17,1},{25,9},{2,18},{10... | collective-permute-start | bytes 1179656 | tf_op jit(solution)/shard_map/ppermute | solution.py:20
  217.8 17.3 %collective-permute-start.23 = (bf16[128,1536]{1,0:T(8,128)(2,1)S(1)}, bf16[128,1536]{1,0:T(8,128)(2,1)S(1)}, u32[]{:S(2)}, u32[]{:S(2)}) collective-permute-start(bf16[128,1536]{1,0:T(8,128)(2,1)S(1)} %collective-permute-done.21.refs_17_), channel_id=1, source_target_pairs={{0,16},{8,24},{16,0},{24,8},{1,17},{9,25},{17,1},{25,9},{2,18},{10... | collective-permute-start | bytes 1179656 | tf_op jit(solution)/shard_map/ppermute | solution.py:20
  218.3 16.8 %collective-permute-start.34 = (bf16[128,1536]{1,0:T(8,128)(2,1)}, bf16[128,1536]{1,0:T(8,128)(2,1)}, u32[]{:S(2)}, u32[]{:S(2)}) collective-permute-start(bf16[128,1536]{1,0:T(8,128)(2,1)} %collective-permute-done.30.refs_19_), channel_id=1, source_target_pairs={{0,1},{1,0},{2,3},{3,2},{4,5},{5,4},{6,7},{7,6},{8,9},{9,8},{10,11... | collective-permute-start | bytes 1179656 | tf_op jit(solution)/shard_map/ppermute | solution.py:20
  228.9 16.9 %collective-permute-start.24 = (bf16[128,1536]{1,0:T(8,128)(2,1)S(1)}, bf16[128,1536]{1,0:T(8,128)(2,1)S(1)}, u32[]{:S(2)}, u32[]{:S(2)}) collective-permute-start(bf16[128,1536]{1,0:T(8,128)(2,1)S(1)} %get-tuple-element.20.refs_16_), channel_id=1, source_target_pairs={{0,1},{1,0},{2,3},{3,2},{4,5},{5,4},{6,7},{7,6},{8,9},{9,8},{10,11... | collective-permute-start | bytes 1179656 | tf_op jit(solution)/shard_map/ppermute | solution.py:20
  229.5 16.3 %collective-permute-start.25 = (bf16[128,1536]{1,0:T(8,128)(2,1)S(1)}, bf16[128,1536]{1,0:T(8,128)(2,1)S(1)}, u32[]{:S(2)}, u32[]{:S(2)}) collective-permute-start(bf16[128,1536]{1,0:T(8,128)(2,1)S(1)} %collective-permute-done.21.refs_17_), channel_id=1, source_target_pairs={{0,1},{1,0},{2,3},{3,2},{4,5},{5,4},{6,7},{7,6},{8,9},{9,8},{10,11... | collective-permute-start | bytes 1179656 | tf_op jit(solution)/shard_map/ppermute | solution.py:20
  229.6 16.2 %collective-permute-start.26 = (bf16[128,1536]{1,0:T(8,128)(2,1)S(1)}, bf16[128,1536]{1,0:T(8,128)(2,1)S(1)}, u32[]{:S(2)}, u32[]{:S(2)}) collective-permute-start(bf16[128,1536]{1,0:T(8,128)(2,1)S(1)} %collective-permute-done.22.refs_18_), channel_id=1, source_target_pairs={{0,1},{1,0},{2,3},{3,2},{4,5},{5,4},{6,7},{7,6},{8,9},{9,8},{10,11... | collective-permute-start | bytes 1179656 | tf_op jit(solution)/shard_map/ppermute | solution.py:20
  (65 other events, 1269.9 us)
